TPU v7x, 32 devices: a whole 2x2x4 slice. The times are simulated.
32 devices in a mesh: tp: 4 (over y, core), ad: 8 (over z, x).
Axes of the slice: x: 2, y: 2, z: 4, core: 2. Of those that a mesh axis runs over, the one named last changes fastest.
Arguments:
- hidden: bfloat16 [2048, 8192], P('ad'), may hold values from -6 to 6
- key_value_weight: bfloat16 [8192, 2048], P(None, 'tp'), may hold values from -0.0625 to 0.0625
- request_group: int32 [2048, 1], P('ad'), may hold values from 0 to 7; in each aligned block of 256 rows (0 to 255, 256 to 511, ...) at most 64 rows name the same one
- request_member: int32 [2048], P('ad'), may hold values from 0 to 3
- adapter_down_weight: bfloat16 [8192, 2048], P('tp', 'ad'), may hold values from -0.0625 to 0.0625
- adapter_up_weight: bfloat16 [2048, 2048], P('ad', 'tp'), may hold values from -0.75 to 0.75
Outputs:
- kv_out: bfloat16 [2048, 2048], P('ad', 'tp')
Inputs may be any that keep to these rules, and one draw needn't show every extreme that they name: `request_group`: among the 256 rows of one index of ad, no group is named by more than 64 rows, a bound that some block reaches.
All inputs are finite; a program needn't handle non-finite values.
Results may differ from a plain program's by a relative error of at most 0.007.
Values may be sent and summed in bfloat16 or wider, within the bound.
No kernel may reach another device: no remote copies, remote signals or barrier semaphores. Data moves between devices by JAX's collectives and lax.ppermute only.
A program may use at most 128 MiB of HBM per device.

v0:
```python
import jax
import jax.numpy as jnp
from jax import lax
from jax.sharding import PartitionSpec as P

ADAPTER_RANK = 64


def shards(
    hidden, key_value_weight, request_group, request_member, adapter_down_weight, adapter_up_weight
):
    column_portion = adapter_down_weight.shape[0]
    adapter_pool_count = adapter_down_weight.shape[1] // ADAPTER_RANK
    base_output = jnp.dot(hidden, key_value_weight, preferred_element_type=jnp.float32)
    own_cols = lax.dynamic_slice_in_dim(
        hidden, lax.axis_index("tp") * column_portion, column_portion, 1
    )
    owner_index = request_group[:, 0]
    adapter = owner_index * adapter_pool_count + request_member
    block_portion = lax.all_gather(adapter_down_weight, "ad", axis=1, tiled=True)
    column_total = block_portion.shape[1]
    scores = jnp.dot(own_cols, block_portion, preferred_element_type=jnp.float32)
    column = jnp.arange(column_total, dtype=jnp.int32)
    kept_mask = (column // ADAPTER_RANK)[None, :] == adapter[:, None]
    selector = (
        (column % ADAPTER_RANK)[:, None] == jnp.arange(ADAPTER_RANK, dtype=jnp.int32)[None, :]
    ).astype(jnp.float32)
    partial_ranks = jnp.dot(
        jnp.where(kept_mask, scores, 0.0), selector, precision=lax.Precision.HIGHEST
    )
    rank_values = lax.psum(partial_ranks, "tp").astype(jnp.bfloat16)
    block_portion = lax.all_gather(adapter_up_weight, "ad", axis=0, tiled=True)
    line_total = block_portion.shape[0]
    row_index = jnp.arange(line_total, dtype=jnp.int32)
    spread = (
        (row_index % ADAPTER_RANK)[None, :] == jnp.arange(ADAPTER_RANK, dtype=jnp.int32)[:, None]
    ).astype(jnp.bfloat16)
    widened = jnp.dot(rank_values, spread, preferred_element_type=jnp.float32)
    kept_mask = (row_index // ADAPTER_RANK)[None, :] == adapter[:, None]
    raised_output = jnp.where(kept_mask, widened, 0.0).astype(jnp.bfloat16)
    adapter_update = jnp.dot(
        raised_output, block_portion, preferred_element_type=jnp.float32
    ).astype(jnp.bfloat16)
    return (base_output + adapter_update.astype(jnp.float32)).astype(jnp.bfloat16)


def solution(mesh):
    placed = (P("ad", None), P(None, "tp"), P("ad", None), P("ad"), P("tp", "ad"), P("ad", "tp"))
    return jax.shard_map(
        shards, mesh=mesh, in_specs=placed, out_specs=P("ad", "tp"), check_vma=False
    )
```

profile of v0, /device:TPU:0, one launch (start us, length us, event | category | flops | bytes accessed | tf_op | source)
XLA Modules:
  0.0 203.6 jit_solution(13971514790394120517)
XLA Ops:
  6.5 0.0 all-gather.3.cloned.1.call-start
  6.5 0.7 all-gather.3.cloned.1.call-update
  7.3 0.0 all-gather.5.cloned.1.call-start
  7.3 0.7 all-gather.5.cloned.1.call-update
  8.0 0.7 broadcast_multiply_fusion
  8.7 0.7 add.34
  9.4 127.7 %all-gather.3.cloned.1.call-done = bf16[2048,2048]{1,0:T(8,128)(2,1)} async-done(((bf16[2048,256]{1,0:T(8,128)(2,1)}), bf16[2048,2048]{1,0:T(8,128)(2,1)}) %all-gather.3.cloned.1.call-update) | async-done | bytes 8388624 | tf_op jit(solution)/shard_map/all_gather | solution.py:20
  137.1 6.1 %compare_select_fusion = f32[256,2048]{1,0:T(8,128)S(1)} fusion(bf16[2048,2048]{1,0:T(8,128)(2,1)} %all-gather.3.cloned.1.call-done, bf16[256,8192]{1,0:T(8,128)(2,1)} %param.6, s32[]{:T(128)S(6)} %select_n.40, s32[2048]{0:T(1024)S(1)} %get-tuple-element.6, s32[256]{0:T(256)S(1)} %add.34), kind=kOutput, calls=%fused_computation.1 | convolution fusion | flops 2148532224 | bytes 11543556 | tf_op jit(solution)/shard_map/dot_general | solution.py:22
  143.1 1.2 fusion.9
  144.4 12.5 %psum.7 = bf16[256,64]{1,0:T(8,128)(2,1)S(1)} all-reduce(f32[256,64]{1,0:T(8,128)S(1)} %fusion.9), channel_id=1, replica_groups=mesh['tp'=4,'ad'=8] {'tp'}, use_global_device_ids=true, to_apply=%region_0.1 | all-reduce | flops 16384 | bytes 98304 | tf_op jit(solution)/shard_map/psum | solution.py:31
  156.9 29.6 %all-gather.5.cloned.1.call-done = bf16[2048,512]{1,0:T(8,128)(2,1)} async-done(((bf16[256,512]{1,0:T(8,128)(2,1)}), bf16[2048,512]{1,0:T(8,128)(2,1)}) %all-gather.5.cloned.1.call-update) | async-done | bytes 2097168 | tf_op jit(solution)/shard_map/all_gather | solution.py:32
  186.5 2.6 %fusion.4 = f32[256,512]{1,0:T(8,128)S(1)} fusion(bf16[2048,512]{1,0:T(8,128)(2,1)} %all-gather.5.cloned.1.call-done, s32[2048]{0:T(1024)S(1)} %get-tuple-element.6, s32[256]{0:T(256)S(1)} %add.34, s32[2048]{0:T(1024)S(1)} %get-tuple-element.5, bf16[256,64]{1,0:T(8,128)(2,1)S(1)} %psum.7), kind=kOutput, calls=%fused_computation.7 | convolution fusion | flops 605945856 | bytes 2671616 | tf_op jit(solution)/shard_map/dot_general | solution.py:41
  189.1 7.7 %fusion.2 = bf16[256,512]{1,0:T(8,128)(2,1)} fusion(f32[256,512]{1,0:T(8,128)S(1)} %fusion.4, bf16[256,8192]{1,0:T(8,128)(2,1)} %param.6, bf16[8192,512]{1,0:T(8,128)(2,1)} %param.7), kind=kOutput, calls=%fused_computation.5 | convolution fusion | flops 2147745792 | bytes 13369344 | tf_op jit(solution)/shard_map/dot_general | solution.py:14
  (1 shorter events, 0.0 us)
Async XLA Ops:
  6.5 130.5 %all-gather.3.cloned.1.call-start = ((), (), s32[]{:S(2)}) async-start(), calls=%async_computation | async-start | bytes 9437184 | tf_op jit(solution)/shard_map/all_gather | solution.py:20
  7.3 179.2 %all-gather.5.cloned.1.call-start = ((), (), s32[]{:S(2)}) async-start(), calls=%async_computation.1 | async-start | bytes 2359296 | tf_op jit(solution)/shard_map/all_gather | solution.py:32
Sparse Core Ops, SparseCore 0:
  9.4 127.6 all-gather.2
  139.2 47.2 all-gather.4
where the time goes:
time: 204 us
  waiting for transfers between devices  159 us (78%)
  matrix products  17.5 us (9%)
  between operations  13.4 us (7%)
  blocking collectives  12.5 us (6%)
    all_gather x1, waiting for transfers between devices, shards(): lax.all_gather(adapter_down_weight, 'ad', axis=1, tiled=True)  128 us
    all_gather x1, waiting for transfers between devices, shards(): block_portion = lax.all_gather(adapter_up_weight, 'ad', axis=0, tiled=True)  29.6 us
    psum x1, blocking collectives, shards(): rank_values = lax.psum(partial_ranks, 'tp').astype(jnp.bfloat16)  12.5 us
    dot_general x1, matrix products, shards(): jnp.dot(hidden, key_value_weight, preferred_element_type=jnp.float32)  7.69 us
    dot_general x1, matrix products, shards(): jnp.dot(own_cols, block_portion, preferred_element_type=jnp.float32)  6.06 us
  transfers between devices with their start and end apart: 2, of which 2 were waited for; matrix products, arithmetic and copies ran while one was open for 4% of the time, Pallas kernels for 0%

commit v1 on v0

--- a/solution.py
+++ b/solution.py
@@ -17,7 +17,7 @@
     )
     owner_index = request_group[:, 0]
     adapter = owner_index * adapter_pool_count + request_member
-    block_portion = lax.all_gather(adapter_down_weight, "ad", axis=1, tiled=True)
+    block_portion = jnp.concatenate(lax.all_gather(adapter_down_weight, "ad"), axis=1)
     column_total = block_portion.shape[1]
     scores = jnp.dot(own_cols, block_portion, preferred_element_type=jnp.float32)
     column = jnp.arange(column_total, dtype=jnp.int32)

time: 204 us -> 204 us (level)
  local copies, waits for them, and re-layouts: 0 us -> 11.5 us
  waiting for transfers between devices: 159 us -> 148 us
    reshape x0 -> x1, local copies, waits for them, and re-layouts: none -> 11.5 us  [shards(): jnp.concatenate(lax.all_gather(adapter_down_weight, 'ad'), axis=1)]
    all_gather x1, waiting for transfers between devices: 29.6 us -> 19.6 us  [shards(): block_portion = lax.all_gather(adapter_up_weight, 'ad', axis=0, tiled=True)]
  transfers between devices with their start and end apart: 2 -> 2, of which waited for: 2 -> 2; matrix products, arithmetic and copies ran while one was open for 4% -> 10% of each run, Pallas kernels for 0% -> 0%
where the time goes in v1:
time: 204 us; the launch traced here: 203 us
  waiting for transfers between devices  148 us (73%)
  matrix products  17.9 us (9%)
  between operations  13.4 us (7%)
  local copies, waits for them, and re-layouts  11.5 us (6%)
  blocking collectives  10.8 us (5%)
    all_gather x1, waiting for transfers between devices, shards(): lax.all_gather(adapter_down_weight, 'ad')  127 us
    all_gather x1, waiting for transfers between devices, shards(): block_portion = lax.all_gather(adapter_up_weight, 'ad', axis=0, tiled=True)  19.6 us
    reshape x1, local copies, waits for them, and re-layouts, shards(): jnp.concatenate(lax.all_gather(adapter_down_weight, 'ad'), axis=1)  11.5 us
    psum x1, blocking collectives, shards(): rank_values = lax.psum(partial_ranks, 'tp').astype(jnp.bfloat16)  10.8 us
    dot_general x1, matrix products, shards(): jnp.dot(hidden, key_value_weight, preferred_element_type=jnp.float32)  7.69 us
    dot_general x1, matrix products, shards(): jnp.dot(own_cols, block_portion, preferred_element_type=jnp.float32)  6.11 us
  transfers between devices with their start and end apart: 2, of which 2 were waited for; matrix products, arithmetic and copies ran while one was open for 10% of the time, Pallas kernels for 0%

profile of v1, /device:TPU:0, one launch (start us, length us, event | category | flops | bytes accessed | tf_op | source)
XLA Modules:
  0.0 203.2 jit_solution(7432913187687295518)
XLA Ops:
  6.5 0.0 all-gather.6.cloned.1.call-start
  6.5 0.7 all-gather.6.cloned.1.call-update
  7.3 0.0 all-gather.4.cloned.1.call-start
  7.3 0.7 all-gather.4.cloned.1.call-update
  8.0 0.7 broadcast_multiply_fusion
  8.7 0.7 add.34
  9.4 127.3 %all-gather.6.cloned.1.call-done = bf16[16384,256]{1,0:T(8,128)(2,1)} async-done(((bf16[2048,256]{1,0:T(8,128)(2,1)}), bf16[16384,256]{1,0:T(8,128)(2,1)}) %all-gather.6.cloned.1.call-update) | async-done | bytes 8388624 | tf_op jit(solution)/shard_map/all_gather | solution.py:20
  136.7 11.5 %copy.7 = bf16[2048,8,256]{0,2,1:T(8,128)(2,1)} copy(bf16[2048,8,256]{2,0,1:T(8,128)(2,1)} %bitcast.11) | data formatting | bytes 16777216 | tf_op jit(solution)/shard_map/reshape | solution.py:20
  148.2 6.1 %compare_select_fusion = f32[256,2048]{1,0:T(8,128)S(1)} fusion(bf16[2048,2048]{0,1:T(8,128)(2,1)} %bitcast.12, bf16[256,8192]{1,0:T(8,128)(2,1)} %param.6, s32[]{:T(128)S(6)} %select_n.40, s32[2048]{0:T(1024)S(1)} %get-tuple-element.6, s32[256]{0:T(256)S(1)} %add.34), kind=kOutput, calls=%fused_computation.1 | convolution fusion | flops 2148532224 | bytes 11543556 | tf_op jit(solution)/shard_map/dot_general | solution.py:22
  154.3 1.5 fusion.9
  155.8 10.8 %psum.7 = bf16[256,64]{0,1:T(8,128)(2,1)S(1)} all-reduce(f32[256,64]{0,1:T(8,128)S(1)} %fusion.9), channel_id=1, replica_groups=mesh['tp'=4,'ad'=8] {'tp'}, use_global_device_ids=true, to_apply=%region_0.1 | all-reduce | flops 16384 | bytes 98304 | tf_op jit(solution)/shard_map/psum | solution.py:31
  166.5 19.6 %all-gather.4.cloned.1.call-done = bf16[2048,512]{1,0:T(8,128)(2,1)} async-done(((bf16[256,512]{1,0:T(8,128)(2,1)}), bf16[2048,512]{1,0:T(8,128)(2,1)}) %all-gather.4.cloned.1.call-update) | async-done | bytes 2097168 | tf_op jit(solution)/shard_map/all_gather | solution.py:32
  186.1 2.6 %fusion.4 = f32[256,512]{1,0:T(8,128)S(1)} fusion(bf16[2048,512]{1,0:T(8,128)(2,1)} %all-gather.4.cloned.1.call-done, s32[2048]{0:T(1024)S(1)} %get-tuple-element.6, s32[256]{0:T(256)S(1)} %add.34, s32[2048]{0:T(1024)S(1)} %get-tuple-element.5, bf16[256,64]{0,1:T(8,128)(2,1)S(1)} %psum.7), kind=kOutput, calls=%fused_computation.7 | convolution fusion | flops 605945856 | bytes 2671616 | tf_op jit(solution)/shard_map/dot_general | solution.py:41
  188.7 7.7 %fusion.2 = bf16[256,512]{1,0:T(8,128)(2,1)} fusion(f32[256,512]{1,0:T(8,128)S(1)} %fusion.4, bf16[256,8192]{1,0:T(8,128)(2,1)} %param.6, bf16[8192,512]{1,0:T(8,128)(2,1)} %param.7), kind=kOutput, calls=%fused_computation.5 | convolution fusion | flops 2147745792 | bytes 13369344 | tf_op jit(solution)/shard_map/dot_general | solution.py:14
  (1 shorter events, 0.0 us)
Async XLA Ops:
  6.5 130.1 %all-gather.6.cloned.1.call-start = ((), (), s32[]{:S(2)}) async-start(), calls=%async_computation.1 | async-start | bytes 9437184 | tf_op jit(solution)/shard_map/all_gather | solution.py:20
  7.3 178.9 %all-gather.4.cloned.1.call-start = ((), (), s32[]{:S(2)}) async-start(), calls=%async_computation | async-start | bytes 2359296 | tf_op jit(solution)/shard_map/all_gather | solution.py:32
Sparse Core Ops, SparseCore 0:
  9.5 127.1 all-gather.5
  138.8 47.2 all-gather.3
